TPU v7x, 128 devices: a whole 4x4x4 slice. The times are simulated.
128 devices in a mesh: section: 2 (over x_lo), expert: 16 (over z, x_hi, core), dp: 4 (over y).
Axes of the slice: x: 4 (x_hi: 2, x_lo: 2; x = x_hi * 2 + x_lo), y: 4, z: 4, core: 2. Of those that a mesh axis runs over, the one named last changes fastest.
Arguments:
- fresh_tokens: bfloat16 [2, 4096, 4096], P(None, ('expert', 'dp')), may hold values from -60 to 60
- in_flight: bfloat16 [4096, 4096], P(('expert', 'dp')), may hold values from -60 to 60
- norm_weight: float32 [2, 4096], P('section'), may hold values from 0.1 to 1.9
- gate_up: bfloat16 [2, 16, 2, 4096, 768], P('section', 'expert', None, 'dp'), may hold values from -0.09375 to 0.09375
- down_proj: bfloat16 [2, 16, 768, 4096], P('section', 'expert', 'dp'), may hold values from -0.21875 to 0.21875
- first_moment: bfloat16 [2, 16, 768, 4096], P('section', 'expert', 'dp'), may hold values from -6 to 6
- second_moment: bfloat16 [2, 16, 768, 4096], P('section', 'expert', 'dp'), may hold values from 0.099609375 to 4
- route_ids: int32 [2, 2, 4096, 8], P('section', None, ('expert', 'dp')), may hold values from 0 to 15, all different within a row; in each aligned block of 64 rows (0 to 63, 64 to 127, ..., all dimensions but the last counted through in order) at most 36 rows name the same one
- route_probs: float32 [2, 2, 4096, 8], P('section', None, ('expert', 'dp')), may hold values from 0.05 to 1
- trade_flags: int32 [8, 1], replicated, may hold values from 0 to 1, as said below
Outputs:
- layer_out: bfloat16 [2, 2, 4096, 4096], P('section', None, ('expert', 'dp'))
- gate_up_moved: bfloat16 [2, 16, 2, 4096, 768], P('section', 'expert', None, 'dp')
- down_moved: bfloat16 [2, 16, 768, 4096], P('section', 'expert', 'dp')
- first_moved: bfloat16 [2, 16, 768, 4096], P('section', 'expert', 'dp')
- second_moved: bfloat16 [2, 16, 768, 4096], P('section', 'expert', 'dp')
Inputs may be any that keep to these rules, and one draw needn't show every extreme that they name: `route_ids`: in each aligned block of 64 rows (one device's tokens of one section and tick) the 8 experts of a token differ and no expert is chosen by more than 36 rows. `trade_flags`: at least one entry is 1 and at least one is 0.
All inputs are finite; a program needn't handle non-finite values.
Results may differ from a plain program's by a relative error of at most 0.0035.
Values may be sent and summed in bfloat16 or wider, within the bound.
A program may use at most 128 MiB of HBM per device.

v0:
```python
import jax
import jax.numpy as jnp
from jax import lax
from jax.sharding import PartitionSpec as P

EXPERTS = 16


def partner(value, axis, bit):
    return lax.ppermute(value, axis, [(i, i ^ 1 << bit) for i in range(lax.axis_size(axis))])


def shifted(block, axis, distance):
    devices = range(lax.axis_size(axis))
    route = [(i - distance, i) for i in devices if i - distance in devices]
    return lax.ppermute(block, axis, route)


def rms_normed(inputs, norm_gain):
    values = inputs.astype(jnp.float32)
    inverse_rms = lax.rsqrt(jnp.mean(values * values, axis=-1, keepdims=True) + 1e-06)
    return (values * inverse_rms * norm_gain).astype(jnp.bfloat16)


def per_device(
    fresh_tokens,
    in_flight,
    norm_weight,
    gate_up,
    down_proj,
    first_moment,
    second_moment,
    route_ids,
    route_probs,
    trade_flags,
):
    groups = lax.axis_size("expert")
    half_span = groups // 2
    top_bit = groups.bit_length() - 2
    own_rank = lax.axis_index("expert")
    section_index = lax.axis_index("section")
    full_gate_up = lax.all_gather(gate_up, "dp", axis=3, tiled=True)
    full_down = lax.all_gather(down_proj, "dp", axis=2, tiled=True)
    gate_weights = full_gate_up[0, 0, 0]
    up_weights = full_gate_up[0, 0, 1]
    down_weights = full_down[0, 0]
    expert_ids = jnp.arange(EXPERTS, dtype=jnp.int32)
    probs = route_probs[0]
    mix = probs / jnp.sum(probs, axis=-1, keepdims=True)
    chosen = route_ids[0][:, :, :, None] == expert_ids
    dense_mix = jnp.sum(jnp.where(chosen, mix[:, :, :, None], 0.0), axis=2)
    all_mix = lax.all_gather(dense_mix, "expert", axis=1, tiled=True)
    own_mix = jnp.sum(jnp.where(expert_ids == own_rank, all_mix, 0.0), axis=-1)
    traded = partner((gate_up, down_proj, first_moment, second_moment), "expert", top_bit)

    def layer(inputs, scale, held=None):
        normed = rms_normed(inputs, norm_weight[0])
        arrived = lax.all_gather(normed, "expert", axis=0, tiled=True)
        gate_part = jnp.dot(arrived, gate_weights, preferred_element_type=jnp.float32)
        up_part = jnp.dot(arrived, up_weights, preferred_element_type=jnp.float32)
        active = (jax.nn.silu(gate_part) * up_part).astype(jnp.bfloat16)
        result = jnp.dot(active, down_weights, preferred_element_type=jnp.float32)
        result = (result * scale[:, None]).astype(jnp.bfloat16)
        if held is not None:
            result, held = lax.optimization_barrier((result, held))
        combined = lax.psum_scatter(result, "expert", scatter_dimension=0, tiled=True)
        return (
            (inputs.astype(jnp.float32) + combined.astype(jnp.float32)).astype(jnp.bfloat16),
            held,
        )

    first_input = jnp.where(section_index == 0, fresh_tokens[0], in_flight)
    tick_zero, traded = layer(first_input, own_mix[0], traded)
    arrived = shifted(tick_zero, "section", 1)
    second_input = jnp.where(section_index == 0, fresh_tokens[1], arrived)
    tick_one, _ = layer(second_input, own_mix[1])
    layer_out = jnp.stack([tick_zero, tick_one])[None]
    own_flags = trade_flags[own_rank % half_span] == 1
    mask_five = own_flags[None, :, None, None, None]
    mask_four = own_flags[None, :, None, None]
    gate_up_moved = jnp.where(mask_five, traded[0], gate_up)
    down_moved = jnp.where(mask_four, traded[1], down_proj)
    first_moved = jnp.where(mask_four, traded[2], first_moment)
    second_moved = jnp.where(mask_four, traded[3], second_moment)
    return (layer_out, gate_up_moved, down_moved, first_moved, second_moved)


def solution(mesh):
    return jax.shard_map(
        per_device,
        mesh=mesh,
        in_specs=(
            P(None, ("expert", "dp"), None),
            P(("expert", "dp"), None),
            P("section", None),
            P("section", "expert", None, "dp", None),
            P("section", "expert", "dp", None),
            P("section", "expert", "dp", None),
            P("section", "expert", "dp", None),
            P("section", None, ("expert", "dp"), None),
            P("section", None, ("expert", "dp"), None),
            P(),
        ),
        out_specs=(
            P("section", None, ("expert", "dp"), None),
            P("section", "expert", None, "dp", None),
            P("section", "expert", "dp", None),
            P("section", "expert", "dp", None),
            P("section", "expert", "dp", None),
        ),
        check_vma=False,
    )
```

profile of v0, /device:TPU:0, one launch (start us, length us, event | category | flops | bytes accessed | tf_op | source)
XLA Modules:
  0.0 780.1 jit_solution(14578231850789856475)
XLA Ops:
  7.2 0.0 all-gather.5.cloned.1.call-start
  7.2 1.3 fusion.6
  8.6 0.0 copy-start.2
  8.6 0.8 copy-done.2
  9.4 1.8 fusion.8
  11.2 0.0 all-gather.5.cloned.1.call-update
  11.2 0.0 all-gather.7.cloned.1.call-start
  11.3 0.7 all-gather.7.cloned.1.call-update
  12.0 0.0 all-gather.9.cloned.1.call-start
  12.0 0.7 all-gather.9.cloned.1.call-update
  12.7 0.0 reduce-scatter.3.cloned.1.call-start
  12.8 4.0 collective-permute-start.1
  16.8 0.0 copy-done
  16.8 0.1 collective-permute-start
  16.9 3.4 collective-permute-start.2
  20.3 0.1 collective-permute-start.3
  20.5 0.0 copy-done.10
  20.5 0.0 copy-done.11
  20.5 0.1 copy.17
  20.6 35.1 %all_gather.18 = f32[2,1024,16]{2,0,1:T(2,128)S(1)} all-gather(f32[2,64,16]{2,0,1:T(2,128)S(1)} %copy.17), channel_id=1, replica_groups=mesh['section'=2,'expert'=16,'dp'=4] {'expert'}, dimensions={1}, use_global_device_ids=true | all-gather | bytes 139264 | tf_op jit(solution)/shard_map/all_gather | solution.py:52
  55.7 1.2 select_reduce_fusion
  56.9 1.1 fusion.15
  58.0 1.2 copy.20
  59.2 187.8 %all-gather.5.cloned.1.call-done = bf16[1024,4096]{1,0:T(8,128)(2,1)} async-done(((bf16[64,4096]{1,0:T(8,128)(2,1)}), bf16[1024,4096]{1,0:T(8,128)(2,1)}) %all-gather.5.cloned.1.call-update) | async-done | bytes 8388624 | tf_op jit(solution)/shard_map/all_gather | solution.py:58
  247.0 118.0 %all-gather.7.cloned.1.call-done = bf16[1,1,2,4096,768]{4,3,2,1,0:T(8,128)(2,1)} async-done(((bf16[1,1,2,1024,768]{4,3,2,1,0:T(8,128)(2,1)}), bf16[1,1,2,4096,768]{4,3,2,1,0:T(8,128)(2,1)}) %all-gather.7.cloned.1.call-update) | async-done | bytes 12582928 | tf_op jit(solution)/shard_map/all_gather | solution.py:42
  365.0 11.0 %fusion.5 = f32[1024,768]{1,0:T(8,128)S(1)} fusion(bf16[1024,4096]{1,0:T(8,128)(2,1)} %all-gather.5.cloned.1.call-done, bf16[1,1,2,4096,768]{4,3,2,1,0:T(8,128)(2,1)} %all-gather.7.cloned.1.call-done), kind=kOutput, calls=%fused_computation.9 | convolution fusion | flops 6442450944 | bytes 17825792 | tf_op jit(solution)/shard_map/dot_general | solution.py:60
  376.0 0.0 copy-done.12
  376.0 0.2 copy-done.13
  376.2 8.1 %multiply_convert_fusion.3 = bf16[1024,768]{1,0:T(8,128)(2,1)} fusion(f32[1024,768]{1,0:T(8,128)S(1)} %fusion.5, bf16[1024,4096]{1,0:T(8,128)(2,1)S(1)} %copy-done.13, bf16[1,1,2,4096,768]{4,3,2,1,0:T(8,128)(2,1)S(1)} %copy-done.12), kind=kOutput, calls=%fused_computation.11 | convolution fusion | flops 6447169536 | bytes 19398656 | tf_op jit(solution)/shard_map/dot_general | solution.py:59
  384.2 49.1 %all-gather.9.cloned.1.call-done = bf16[1,1,768,4096]{3,2,1,0:T(8,128)(2,1)} async-done(((bf16[1,1,192,4096]{3,2,1,0:T(8,128)(2,1)}), bf16[1,1,768,4096]{3,2,1,0:T(8,128)(2,1)}) %all-gather.9.cloned.1.call-update) | async-done | bytes 6291472 | tf_op jit(solution)/shard_map/all_gather | solution.py:43
  433.4 11.2 %multiply_convert_fusion.1 = bf16[1024,4096]{1,0:T(8,128)(2,1)} fusion(f32[1024]{0:T(1024)S(1)} %bitcast.45, bf16[1024,768]{1,0:T(8,128)(2,1)} %multiply_convert_fusion.3, bf16[1,1,768,4096]{3,2,1,0:T(8,128)(2,1)} %all-gather.9.cloned.1.call-done), kind=kOutput, calls=%fused_computation.1 | convolution fusion | flops 6450839552 | bytes 16257024 | tf_op jit(solution)/shard_map/dot_general | solution.py:62
  444.6 0.0 collective-permute-done.2
  444.6 0.0 collective-permute-done.3
  444.6 0.0 collective-permute-done.1
  444.6 0.0 collective-permute-done
  444.6 0.0 reduce-scatter.3.cloned.1.call-update
  444.7 0.0 copy-start.9
  444.7 0.0 all-gather.11.cloned.1.call-start
  444.7 103.2 %reduce-scatter.3.cloned.1.call-done = bf16[64,4096]{1,0:T(8,128)(2,1)} async-done(((bf16[1024,4096]{1,0:T(8,128)(2,1)}), bf16[64,4096]{1,0:T(8,128)(2,1)}) %reduce-scatter.3.cloned.1.call-update) | async-done | bytes 524304 | tf_op jit(solution)/shard_map/reduce_scatter | solution.py:66
  547.9 1.3 fusion.9
  549.3 0.0 copy-start.5
  549.3 2.5 collective-permute-start.4
  551.8 10.1 %collective-permute-done.4 = bf16[64,4096]{1,0:T(8,128)(2,1)S(1)} collective-permute-done((bf16[64,4096]{1,0:T(8,128)(2,1)S(1)}, bf16[64,4096]{1,0:T(8,128)(2,1)S(1)}, u32[]{:S(2)}, u32[]{:S(2)}) %collective-permute-start.4) | collective-permute-done | bytes 524320 | tf_op jit(solution)/shard_map/ppermute | solution.py:16
  561.9 1.3 fusion.10
  563.2 0.8 copy-done.3
  564.0 1.0 fusion.12
  565.0 0.0 all-gather.11.cloned.1.call-update
  565.0 0.2 reduce-scatter.5.cloned.1.call-start
  565.3 1.2 copy.21
  566.5 71.6 %all-gather.11.cloned.1.call-done = bf16[1024,4096]{1,0:T(8,128)(2,1)} async-done(((bf16[64,4096]{1,0:T(8,128)(2,1)}), bf16[1024,4096]{1,0:T(8,128)(2,1)}) %all-gather.11.cloned.1.call-update) | async-done | bytes 8388624 | tf_op jit(solution)/shard_map/all_gather | solution.py:58
  638.1 11.0 %fusion.4 = f32[1024,768]{1,0:T(8,128)S(1)} fusion(bf16[1024,4096]{1,0:T(8,128)(2,1)} %all-gather.11.cloned.1.call-done, bf16[1,1,2,4096,768]{4,3,2,1,0:T(8,128)(2,1)} %all-gather.7.cloned.1.call-done), kind=kOutput, calls=%fused_computation.8 | convolution fusion | flops 6442450944 | bytes 17825792 | tf_op jit(solution)/shard_map/dot_general | solution.py:60
  649.1 9.8 %multiply_convert_fusion.2 = bf16[1024,768]{1,0:T(8,128)(2,1)S(1)} fusion(f32[1024,768]{1,0:T(8,128)S(1)} %fusion.4, bf16[1024,4096]{1,0:T(8,128)(2,1)S(1)} %copy-done.14, bf16[1,1,2,4096,768]{4,3,2,1,0:T(8,128)(2,1)} %all-gather.7.cloned.1.call-done), kind=kOutput, calls=%fused_computation.10 | convolution fusion | flops 6447169536 | bytes 19398656 | tf_op jit(solution)/shard_map/dot_general | solution.py:59
  658.9 11.7 %multiply_convert_fusion = bf16[1024,4096]{1,0:T(8,128)(2,1)} fusion(f32[1024]{0:T(1024)S(1)} %bitcast.46, bf16[1024,768]{1,0:T(8,128)(2,1)S(1)} %multiply_convert_fusion.2, bf16[1,1,768,4096]{3,2,1,0:T(8,128)(2,1)} %all-gather.9.cloned.1.call-done), kind=kOutput, calls=%fused_computation | convolution fusion | flops 6450839552 | bytes 16257024 | tf_op jit(solution)/shard_map/dot_general | solution.py:62
  670.7 0.0 reduce-scatter.5.cloned.1.call-update
  670.7 0.6 copy-done.15
  671.3 0.6 fusion.16
  671.9 4.6 broadcast_select_fusion
  676.6 4.0 broadcast_select_fusion.3
  680.5 0.0 copy-done.7
  680.5 4.9 broadcast_select_fusion.1
  685.4 85.6 %reduce-scatter.5.cloned.1.call-done = bf16[64,4096]{1,0:T(8,128)(2,1)} async-done(((bf16[1024,4096]{1,0:T(8,128)(2,1)}), bf16[64,4096]{1,0:T(8,128)(2,1)}) %reduce-scatter.5.cloned.1.call-update) | async-done | bytes 524304 | tf_op jit(solution)/shard_map/reduce_scatter | solution.py:66
  771.0 0.0 copy-done.4
  771.0 1.2 fusion.14
  772.2 1.1 maximum_bitcast_fusion
  (25 shorter events, 0.1 us)
Async XLA Ops:
  7.2 239.8 %all-gather.5.cloned.1.call-start = ((), (), s32[]{:S(2)}) async-start(), calls=%async_computation.2 | async-start | bytes 8912896 | tf_op jit(solution)/shard_map/all_gather | solution.py:58
  8.6 0.8 copy-start.2
  9.4 7.5 copy-start
  9.4 11.1 %copy-start.10 = (f32[1,2,64,8]{2,3,1,0:T(8,128)S(1)}, f32[1,2,64,8]{2,3,1,0:T(8,128)}, u32[]{:S(2)}) copy-start(f32[1,2,64,8]{2,3,1,0:T(8,128)} %param.18) | copy-start | bytes 12292
  9.4 11.1 %copy-start.11 = (s32[1,2,64,8]{2,3,1,0:T(8,128)S(1)}, s32[1,2,64,8]{2,3,1,0:T(8,128)}, u32[]{:S(2)}) copy-start(s32[1,2,64,8]{2,3,1,0:T(8,128)} %param.17) | copy-start | bytes 12292
  11.2 353.7 %all-gather.7.cloned.1.call-start = ((), (), s32[]{:S(2)}) async-start(), calls=%async_computation.3 | async-start | bytes 15728640 | tf_op jit(solution)/shard_map/all_gather | solution.py:42
  12.0 421.4 %all-gather.9.cloned.1.call-start = ((), (), s32[]{:S(2)}) async-start(), calls=%async_computation.4 | async-start | bytes 7864320 | tf_op jit(solution)/shard_map/all_gather | solution.py:43
  12.7 535.2 %reduce-scatter.3.cloned.1.call-start = ((), (), s32[]{:S(2)}) async-start(), calls=%async_computation.5 | async-start | bytes 8912896 | tf_op jit(solution)/shard_map/reduce_scatter | solution.py:66
  12.8 431.9 %collective-permute-start.1 = (bf16[1,1,192,4096]{3,2,1,0:T(8,128)(2,1)}, bf16[1,1,192,4096]{3,2,1,0:T(8,128)(2,1)}, u32[]{:S(2)}, u32[]{:S(2)}) collective-permute-start(bf16[1,1,192,4096]{3,2,1,0:T(8,128)(2,1)} %param.14), channel_id=1, source_target_pairs={{0,32},{4,36},{8,40},{12,44},{16,48},{20,52},{24,56},{28,60},{32,0... | collective-permute-start | bytes 4718600 | tf_op jit(solution)/shard_map/ppermute | solution.py:10
  16.8 427.8 %collective-permute-start = (bf16[1,1,2,1024,768]{4,3,2,1,0:T(8,128)(2,1)S(1)}, bf16[1,1,2,1024,768]{4,3,2,1,0:T(8,128)(2,1)}, u32[]{:S(2)}, u32[]{:S(2)}) collective-permute-start(bf16[1,1,2,1024,768]{4,3,2,1,0:T(8,128)(2,1)S(1)} %copy-done), channel_id=1, source_target_pairs={{0,32},{4,36},{8,40},{12,44},{16,48},{20,52},{24,56},{28,60},{32,0... | collective-permute-start | bytes 9437192 | tf_op jit(solution)/shard_map/ppermute | solution.py:10
  16.9 427.7 %collective-permute-start.2 = (bf16[1,1,192,4096]{3,2,1,0:T(8,128)(2,1)}, bf16[1,1,192,4096]{3,2,1,0:T(8,128)(2,1)}, u32[]{:S(2)}, u32[]{:S(2)}) collective-permute-start(bf16[1,1,192,4096]{3,2,1,0:T(8,128)(2,1)} %param.15), channel_id=1, source_target_pairs={{0,32},{4,36},{8,40},{12,44},{16,48},{20,52},{24,56},{28,60},{32,0... | collective-permute-start | bytes 4718600 | tf_op jit(solution)/shard_map/ppermute | solution.py:10
  20.3 424.3 %collective-permute-start.3 = (bf16[1,1,192,4096]{3,2,1,0:T(8,128)(2,1)}, bf16[1,1,192,4096]{3,2,1,0:T(8,128)(2,1)}, u32[]{:S(2)}, u32[]{:S(2)}) collective-permute-start(bf16[1,1,192,4096]{3,2,1,0:T(8,128)(2,1)} %param.16), channel_id=1, source_target_pairs={{0,32},{4,36},{8,40},{12,44},{16,48},{20,52},{24,56},{28,60},{32,0... | collective-permute-start | bytes 4718600 | tf_op jit(solution)/shard_map/ppermute | solution.py:10
  365.0 11.0 %copy-start.12 = (bf16[1,1,2,4096,768]{4,3,2,1,0:T(8,128)(2,1)S(1)}, bf16[1,1,2,4096,768]{4,3,2,1,0:T(8,128)(2,1)}, u32[]{:S(2)}) copy-start(bf16[1,1,2,4096,768]{4,3,2,1,0:T(8,128)(2,1)} %all-gather.7.cloned.1.call-done) | copy-start | bytes 37748740
  365.0 11.2 %copy-start.13 = (bf16[1024,4096]{1,0:T(8,128)(2,1)S(1)}, bf16[1024,4096]{1,0:T(8,128)(2,1)}, u32[]{:S(2)}) copy-start(bf16[1024,4096]{1,0:T(8,128)(2,1)} %all-gather.5.cloned.1.call-done) | copy-start | bytes 25165828
  444.7 119.3 %copy-start.9 = (f32[1,4096]{1,0:T(1,128)S(1)}, f32[1,4096]{1,0:T(1,128)}, u32[]{:S(2)}) copy-start(f32[1,4096]{1,0:T(1,128)} %param.12) | copy-start | bytes 49156
  444.7 193.4 %all-gather.11.cloned.1.call-start = ((), (), s32[]{:S(2)}) async-start(), calls=%async_computation.6 | async-start | bytes 8912896 | tf_op jit(solution)/shard_map/all_gather | solution.py:58
  549.3 2.5 copy-start.5
  549.3 12.6 %collective-permute-start.4 = (bf16[64,4096]{1,0:T(8,128)(2,1)S(1)}, bf16[64,4096]{1,0:T(8,128)(2,1)S(1)}, u32[]{:S(2)}, u32[]{:S(2)}) collective-permute-start(bf16[64,4096]{1,0:T(8,128)(2,1)S(1)} %fusion.9), channel_id=1, source_target_pairs={{0,64},{1,65},{2,66},{3,67},{4,68},{5,69},{6,70},{7,71},{8,72},{9,... | collective-permute-start | bytes 1572872 | tf_op jit(solution)/shard_map/ppermute | solution.py:16
  563.2 0.8 copy-start.3
  565.0 206.0 %reduce-scatter.5.cloned.1.call-start = ((), (), s32[]{:S(2)}) async-start(), calls=%async_computation.7 | async-start | bytes 8912896 | tf_op jit(solution)/shard_map/reduce_scatter | solution.py:66
  638.1 11.1 %copy-start.14 = (bf16[1024,4096]{1,0:T(8,128)(2,1)S(1)}, bf16[1024,4096]{1,0:T(8,128)(2,1)}, u32[]{:S(2)}) copy-start(bf16[1024,4096]{1,0:T(8,128)(2,1)} %all-gather.11.cloned.1.call-done) | copy-start | bytes 25165828
  670.7 0.7 copy-start.15
  671.9 4.7 copy-start.1
  676.6 4.0 copy-start.7
  676.6 4.0 copy-start.8
  680.5 90.5 %copy-start.4 = (bf16[64,4096]{1,0:T(8,128)(2,1)S(1)}, bf16[64,4096]{1,0:T(8,128)(2,1)}, u32[]{:S(2)}) copy-start(bf16[64,4096]{1,0:T(8,128)(2,1)} %copy-done.3) | copy-start | bytes 1572868
  680.5 91.6 %copy-start.6 = (bf16[64,4096]{1,0:T(8,128)(2,1)S(1)}, bf16[64,4096]{1,0:T(8,128)(2,1)}, u32[]{:S(2)}) copy-start(bf16[64,4096]{1,0:T(8,128)(2,1)} %copy-done.5) | copy-start | bytes 1572868
Sparse Core Ops, SparseCore 0:
  11.4 235.5 all-gather.4
  248.6 116.2 all-gather.6
  366.6 66.6 all-gather.8
  444.8 103.1 reduce-scatter.2
  565.1 72.8 all-gather.10
  670.8 100.1 reduce-scatter.4
where the time goes:
time: 781 us; the launch traced here: 780 us
  waiting for transfers between devices  627 us (80%)
  matrix products  62.9 us (8%)
  blocking collectives  35.1 us (4%)
  other arithmetic  24.4 us (3%)
  between operations  14.3 us (2%)
  starting transfers between devices  10.6 us (1%)
    all_gather x2, waiting for transfers between devices, layer(): arrived = lax.all_gather(normed, 'expert', axis=0, tiled=True)  259 us
    reduce_scatter x2, waiting for transfers between devices, layer(): lax.psum_scatter(result, 'expert', scatter_dimension=0, tiled=True)  189 us
    all_gather x1, waiting for transfers between devices, per_device(): full_gate_up = lax.all_gather(gate_up, 'dp', axis=3, tiled=True)  118 us
    all_gather x1, waiting for transfers between devices, per_device(): full_down = lax.all_gather(down_proj, 'dp', axis=2, tiled=True)  49.1 us
    all_gather x1, blocking collectives, per_device(): all_mix = lax.all_gather(dense_mix, 'expert', axis=1, tiled=True)  35.1 us
    dot_general x2, matrix products, layer(): result = jnp.dot(active, down_weights, preferred_element_type=jnp.float32)  23 us
    dot_general x2, matrix products, layer(): up_part = jnp.dot(arrived, up_weights, preferred_element_type=jnp.float32)  22.1 us
    dot_general x2, matrix products, layer(): jnp.dot(arrived, gate_weights, preferred_element_type=jnp.float32)  17.8 us
  transfers between devices with their start and end apart: 11, of which 7 were waited for; matrix products, arithmetic and copies ran while one was open for 6% of the time, Pallas kernels for 0%

commit v1 on v0

--- a/solution.py
+++ b/solution.py
@@ -55,7 +55,15 @@
 
     def layer(inputs, scale, held=None):
         normed = rms_normed(inputs, norm_weight[0])
-        arrived = lax.all_gather(normed, "expert", axis=0, tiled=True)
+        arrived = jnp.concatenate(
+            lax.all_to_all(
+                jnp.stack([normed for _ in range(lax.axis_size("expert"))], 0),
+                split_axis=0,
+                axis_name="expert",
+                concat_axis=0,
+            ),
+            0,
+        )
         gate_part = jnp.dot(arrived, gate_weights, preferred_element_type=jnp.float32)
         up_part = jnp.dot(arrived, up_weights, preferred_element_type=jnp.float32)
         active = (jax.nn.silu(gate_part) * up_part).astype(jnp.bfloat16)

time: 781 us -> 687 us (0.88)
  waiting for transfers between devices: 627 us -> 437 us
  blocking collectives: 35.1 us -> 109 us
  starting transfers between devices: 10.6 us -> 23.1 us
  local copies, waits for them, and re-layouts: 6.06 us -> 14.9 us
    all_gather x2 -> x0, waiting for transfers between devices: 259 us -> none  [layer(): arrived = lax.all_gather(normed, 'expert', axis=0, tiled=True)]
    all_gather x1, waiting for transfers between devices: 118 us -> 0.01 us  [per_device(): full_gate_up = lax.all_gather(gate_up, 'dp', axis=3, tiled=True)]
    all_to_all x0 -> x2, waiting for transfers between devices: none -> 95.3 us  [layer(): lax.all_to_all(jnp.stack([normed for _ in range(lax.axis_size('expert'))]...]
    ppermute x4, waiting for transfers between devices: 0.01 us -> 81.4 us  [partner(): lax.ppermute(value, axis, [(i, i ^ 1 << bit) for i in range(lax.axis_size...]
    all_gather x1, blocking collectives: 35.1 us -> 109 us  [per_device(): all_mix = lax.all_gather(dense_mix, 'expert', axis=1, tiled=True)]
    reduce_scatter x2, waiting for transfers between devices: 189 us -> 215 us  [layer(): lax.psum_scatter(result, 'expert', scatter_dimension=0, tiled=True)]
    all_gather x1, waiting for transfers between devices: 49.1 us -> 34.2 us  [per_device(): full_down = lax.all_gather(down_proj, 'dp', axis=2, tiled=True)]
    all_to_all x0 -> x2, starting transfers between devices: none -> 13.1 us  [layer(): lax.all_to_all(jnp.stack([normed for _ in range(lax.axis_size('expert'))]...]
  transfers between devices with their start and end apart: 11 -> 11, of which waited for: 7 -> 7; matrix products, arithmetic and copies ran while one was open for 6% -> 8% of each run, Pallas kernels for 0% -> 0%
where the time goes in v1:
time: 687 us; the launch traced here: 686 us
  waiting for transfers between devices  437 us (64%)
  blocking collectives  109 us (16%)
  matrix products  67.5 us (10%)
  starting transfers between devices  23.1 us (3%)
  other arithmetic  21 us (3%)
  local copies, waits for them, and re-layouts  14.9 us (2%)
  between operations  14 us (2%)
    reduce_scatter x2, waiting for transfers between devices, layer(): lax.psum_scatter(result, 'expert', scatter_dimension=0, tiled=True)  215 us
    all_gather x1, blocking collectives, per_device(): all_mix = lax.all_gather(dense_mix, 'expert', axis=1, tiled=True)  109 us
    all_to_all x2, waiting for transfers between devices, layer(): lax.all_to_all(jnp.stack([normed for _ in range(lax.axis_size('expert'))]...  95.3 us
    ppermute x4, waiting for transfers between devices, partner(): lax.ppermute(value, axis, [(i, i ^ 1 << bit) for i in range(lax.axis_size...  81.4 us
    all_gather x1, waiting for transfers between devices, per_device(): full_down = lax.all_gather(down_proj, 'dp', axis=2, tiled=True)  34.2 us
    dot_general x2, matrix products, layer(): result = jnp.dot(active, down_weights, preferred_element_type=jnp.float32)  23 us
    dot_general x2, matrix products, layer(): up_part = jnp.dot(arrived, up_weights, preferred_element_type=jnp.float32)  23 us
    dot_general x2, matrix products, layer(): jnp.dot(arrived, gate_weights, preferred_element_type=jnp.float32)  21.6 us
  transfers between devices with their start and end apart: 11, of which 7 were waited for; matrix products, arithmetic and copies ran while one was open for 8% of the time, Pallas kernels for 0%

profile of v1, /device:TPU:0, one launch (start us, length us, event | category | flops | bytes accessed | tf_op | source)
XLA Modules:
  0.0 686.0 jit_solution(11759080795299822149)
XLA Ops:
  7.2 0.0 copy-start.9
  7.2 0.0 copy-start.10
  7.2 0.0 copy-start.11
  7.2 0.0 all-gather.3.cloned.1.call-start
  7.2 0.7 all-gather.3.cloned.1.call-update
  7.9 0.5 copy-done.9
  8.4 0.1 copy-done.10
  8.5 0.3 fusion.6
  8.8 0.0 copy-start.2
  8.8 0.2 fusion.8
  9.0 0.6 copy-done.2
  9.6 4.3 stack.10
  13.9 8.3 %all-to-all-start = ((bf16[16,64,4096]{2,1,0:T(8,128)(2,1)}), bf16[16,64,4096]{2,1,0:T(8,128)(2,1)}, u32[]{:S(2)}, u32[]{:S(2)}) async-start(bf16[16,64,4096]{2,1,0:T(8,128)(2,1)} %stack.10), calls=%async_computation | async-start | bytes 16777216 | tf_op jit(solution)/shard_map/all_to_all | solution.py:59
  22.2 0.0 all-gather.5.cloned.1.call-start
  22.3 0.7 all-gather.5.cloned.1.call-update
  23.0 0.0 reduce-scatter.3.cloned.1.call-start
  23.0 3.5 collective-permute-start.1
  26.5 0.2 collective-permute-start
  26.6 3.4 collective-permute-start.2
  30.0 0.2 collective-permute-start.3
  30.2 0.0 copy-done.12
  30.2 0.1 copy.17
  30.3 108.6 %all_gather.11 = f32[2,1024,16]{2,0,1:T(2,128)S(1)} all-gather(f32[2,64,16]{2,0,1:T(2,128)S(1)} %copy.17), channel_id=1, replica_groups=mesh['section'=2,'expert'=16,'dp'=4] {'expert'}, dimensions={1}, use_global_device_ids=true | all-gather | bytes 139264 | tf_op jit(solution)/shard_map/all_gather | solution.py:52
  139.0 1.2 select_reduce_fusion
  140.1 1.1 fusion.15
  141.2 1.3 copy.20
  142.5 0.0 all-to-all-done
  142.5 0.0 all-gather.3.cloned.1.call-done
  142.5 12.1 %fusion.5 = f32[1024,768]{1,0:T(8,128)S(1)} fusion(bf16[1024,4096]{1,0:T(8,128)(2,1)} %bitcast.2, bf16[1,1,2,4096,768]{4,3,2,1,0:T(8,128)(2,1)} %all-gather.3.cloned.1.call-done), kind=kOutput, calls=%fused_computation.9 | convolution fusion | flops 6442450944 | bytes 17825792 | tf_op jit(solution)/shard_map/dot_general | solution.py:68
  154.6 0.0 copy-done.14
  154.6 10.4 %multiply_convert_fusion.3 = bf16[1024,768]{1,0:T(8,128)(2,1)} fusion(f32[1024,768]{1,0:T(8,128)S(1)} %fusion.5, bf16[1024,4096]{1,0:T(8,128)(2,1)} %bitcast.2, bf16[1,1,2,4096,768]{4,3,2,1,0:T(8,128)(2,1)S(1)} %copy-done.14), kind=kOutput, calls=%fused_computation.11 | convolution fusion | flops 6447169536 | bytes 19398656 | tf_op jit(solution)/shard_map/dot_general | solution.py:67
  165.0 34.2 %all-gather.5.cloned.1.call-done = bf16[1,1,768,4096]{3,2,1,0:T(8,128)(2,1)} async-done(((bf16[1,1,192,4096]{3,2,1,0:T(8,128)(2,1)}), bf16[1,1,768,4096]{3,2,1,0:T(8,128)(2,1)}) %all-gather.5.cloned.1.call-update) | async-done | bytes 6291472 | tf_op jit(solution)/shard_map/all_gather | solution.py:43
  199.2 11.3 %multiply_convert_fusion.1 = bf16[1024,4096]{1,0:T(8,128)(2,1)} fusion(f32[1024]{0:T(1024)S(1)} %bitcast.47, bf16[1024,768]{1,0:T(8,128)(2,1)} %multiply_convert_fusion.3, bf16[1,1,768,4096]{3,2,1,0:T(8,128)(2,1)} %all-gather.5.cloned.1.call-done), kind=kOutput, calls=%fused_computation.1 | convolution fusion | flops 6450839552 | bytes 16257024 | tf_op jit(solution)/shard_map/dot_general | solution.py:70
  210.4 48.1 %collective-permute-done.2 = bf16[1,1,192,4096]{3,2,1,0:T(8,128)(2,1)} collective-permute-done((bf16[1,1,192,4096]{3,2,1,0:T(8,128)(2,1)}, bf16[1,1,192,4096]{3,2,1,0:T(8,128)(2,1)}, u32[]{:S(2)}, u32[]{:S(2)}) %collective-permute-start.2) | collective-permute-done | bytes 1572896 | tf_op jit(solution)/shard_map/ppermute | solution.py:10
  258.6 33.2 %collective-permute-done.3 = bf16[1,1,192,4096]{3,2,1,0:T(8,128)(2,1)} collective-permute-done((bf16[1,1,192,4096]{3,2,1,0:T(8,128)(2,1)}, bf16[1,1,192,4096]{3,2,1,0:T(8,128)(2,1)}, u32[]{:S(2)}, u32[]{:S(2)}) %collective-permute-start.3) | collective-permute-done | bytes 1572896 | tf_op jit(solution)/shard_map/ppermute | solution.py:10
  291.8 0.0 collective-permute-done.1
  291.8 0.0 collective-permute-done
  291.8 0.0 reduce-scatter.3.cloned.1.call-update
  291.8 127.6 %reduce-scatter.3.cloned.1.call-done = bf16[64,4096]{1,0:T(8,128)(2,1)} async-done(((bf16[1024,4096]{1,0:T(8,128)(2,1)}), bf16[64,4096]{1,0:T(8,128)(2,1)}) %reduce-scatter.3.cloned.1.call-update) | async-done | bytes 524304 | tf_op jit(solution)/shard_map/reduce_scatter | solution.py:74
  419.4 1.3 fusion.9
  420.8 2.5 collective-permute-start.4
  423.3 10.1 %collective-permute-done.4 = bf16[64,4096]{1,0:T(8,128)(2,1)S(1)} collective-permute-done((bf16[64,4096]{1,0:T(8,128)(2,1)S(1)}, bf16[64,4096]{1,0:T(8,128)(2,1)S(1)}, u32[]{:S(2)}, u32[]{:S(2)}) %collective-permute-start.4) | collective-permute-done | bytes 524320 | tf_op jit(solution)/shard_map/ppermute | solution.py:16
  433.4 1.3 fusion.10
  434.7 0.0 copy-start.3
  434.7 0.8 copy-done.3
  435.5 0.2 fusion.12
  435.7 4.3 stack.12
  440.0 4.8 all-to-all-start.1
  444.8 0.3 reduce-scatter.5.cloned.1.call-start
  445.1 1.2 copy.21
  446.3 95.3 %all-to-all-done.1 = bf16[16,64,4096]{2,1,0:T(8,128)(2,1)} async-done(((bf16[16,64,4096]{2,1,0:T(8,128)(2,1)}), bf16[16,64,4096]{2,1,0:T(8,128)(2,1)}, u32[]{:S(2)}, u32[]{:S(2)}) %all-to-all-start.1) | async-done | bytes 8388640 | tf_op jit(solution)/shard_map/all_to_all | solution.py:59
  541.5 10.9 %fusion.4 = f32[1024,768]{1,0:T(8,128)S(1)} fusion(bf16[1024,4096]{1,0:T(8,128)(2,1)} %bitcast.11, bf16[1,1,2,4096,768]{4,3,2,1,0:T(8,128)(2,1)} %all-gather.3.cloned.1.call-done), kind=kOutput, calls=%fused_computation.8 | convolution fusion | flops 6442450944 | bytes 17825792 | tf_op jit(solution)/shard_map/dot_general | solution.py:68
  552.5 11.2 %multiply_convert_fusion.2 = bf16[1024,768]{1,0:T(8,128)(2,1)S(1)} fusion(f32[1024,768]{1,0:T(8,128)S(1)} %fusion.4, bf16[1024,4096]{1,0:T(8,128)(2,1)} %bitcast.11, bf16[1,1,2,4096,768]{4,3,2,1,0:T(8,128)(2,1)} %all-gather.3.cloned.1.call-done), kind=kOutput, calls=%fused_computation.10 | convolution fusion | flops 6447169536 | bytes 19398656 | tf_op jit(solution)/shard_map/dot_general | solution.py:67
  563.7 11.7 %multiply_convert_fusion = bf16[1024,4096]{1,0:T(8,128)(2,1)} fusion(f32[1024]{0:T(1024)S(1)} %bitcast.48, bf16[1024,768]{1,0:T(8,128)(2,1)S(1)} %multiply_convert_fusion.2, bf16[1,1,768,4096]{3,2,1,0:T(8,128)(2,1)} %all-gather.5.cloned.1.call-done), kind=kOutput, calls=%fused_computation | convolution fusion | flops 6450839552 | bytes 16257024 | tf_op jit(solution)/shard_map/dot_general | solution.py:70
  575.4 0.0 reduce-scatter.5.cloned.1.call-update
  575.5 0.6 copy-done.15
  576.1 0.6 fusion.16
  576.7 4.6 broadcast_select_fusion
  581.3 4.0 broadcast_select_fusion.3
  585.4 0.0 copy-done.7
  585.4 4.9 broadcast_select_fusion.1
  590.3 86.9 %reduce-scatter.5.cloned.1.call-done = bf16[64,4096]{1,0:T(8,128)(2,1)} async-done(((bf16[1024,4096]{1,0:T(8,128)(2,1)}), bf16[64,4096]{1,0:T(8,128)(2,1)}) %reduce-scatter.5.cloned.1.call-update) | async-done | bytes 524304 | tf_op jit(solution)/shard_map/reduce_scatter | solution.py:74
  677.2 1.2 fusion.14
  678.4 1.1 maximum_bitcast_fusion
  (25 shorter events, 0.1 us)
Async XLA Ops:
  7.2 1.2 copy-start.9
  7.2 1.3 copy-start.10
  7.2 1.7 copy-start.11
  7.2 135.3 %all-gather.3.cloned.1.call-start = ((), (), s32[]{:S(2)}) async-start(), calls=%async_computation.4 | async-start | bytes 15728640 | tf_op jit(solution)/shard_map/all_gather | solution.py:42
  8.8 0.8 copy-start.2
  13.9 12.5 %copy-start = (bf16[1,1,2,1024,768]{4,3,2,1,0:T(8,128)(2,1)S(1)}, bf16[1,1,2,1024,768]{4,3,2,1,0:T(8,128)(2,1)}, u32[]{:S(2)}) copy-start(bf16[1,1,2,1024,768]{4,3,2,1,0:T(8,128)(2,1)} %param.13) | copy-start | bytes 9437188
  13.9 16.2 %copy-start.12 = (f32[1,2,64,8]{2,3,1,0:T(8,128)S(1)}, f32[1,2,64,8]{2,3,1,0:T(8,128)}, u32[]{:S(2)}) copy-start(f32[1,2,64,8]{2,3,1,0:T(8,128)} %param.18) | copy-start | bytes 12292
  13.9 16.3 %copy-start.13 = (s32[1,2,64,8]{2,3,1,0:T(8,128)S(1)}, s32[1,2,64,8]{2,3,1,0:T(8,128)}, u32[]{:S(2)}) copy-start(s32[1,2,64,8]{2,3,1,0:T(8,128)} %param.17) | copy-start | bytes 12292
  13.9 128.6 %all-to-all-start = ((bf16[16,64,4096]{2,1,0:T(8,128)(2,1)}), bf16[16,64,4096]{2,1,0:T(8,128)(2,1)}, u32[]{:S(2)}, u32[]{:S(2)}) async-start(bf16[16,64,4096]{2,1,0:T(8,128)(2,1)} %stack.10), calls=%async_computation | async-start | bytes 16777216 | tf_op jit(solution)/shard_map/all_to_all | solution.py:59
  22.2 177.0 %all-gather.5.cloned.1.call-start = ((), (), s32[]{:S(2)}) async-start(), calls=%async_computation.5 | async-start | bytes 7864320 | tf_op jit(solution)/shard_map/all_gather | solution.py:43
  23.0 396.4 %reduce-scatter.3.cloned.1.call-start = ((), (), s32[]{:S(2)}) async-start(), calls=%async_computation.6 | async-start | bytes 8912896 | tf_op jit(solution)/shard_map/reduce_scatter | solution.py:74
  23.0 268.8 %collective-permute-start.1 = (bf16[1,1,192,4096]{3,2,1,0:T(8,128)(2,1)}, bf16[1,1,192,4096]{3,2,1,0:T(8,128)(2,1)}, u32[]{:S(2)}, u32[]{:S(2)}) collective-permute-start(bf16[1,1,192,4096]{3,2,1,0:T(8,128)(2,1)} %param.14), channel_id=1, source_target_pairs={{0,32},{4,36},{8,40},{12,44},{16,48},{20,52},{24,56},{28,60},{32,0... | collective-permute-start | bytes 4718600 | tf_op jit(solution)/shard_map/ppermute | solution.py:10
  26.5 265.3 %collective-permute-start = (bf16[1,1,2,1024,768]{4,3,2,1,0:T(8,128)(2,1)S(1)}, bf16[1,1,2,1024,768]{4,3,2,1,0:T(8,128)(2,1)}, u32[]{:S(2)}, u32[]{:S(2)}) collective-permute-start(bf16[1,1,2,1024,768]{4,3,2,1,0:T(8,128)(2,1)S(1)} %copy-done), channel_id=1, source_target_pairs={{0,32},{4,36},{8,40},{12,44},{16,48},{20,52},{24,56},{28,60},{32,0... | collective-permute-start | bytes 9437192 | tf_op jit(solution)/shard_map/ppermute | solution.py:10
  26.6 231.9 %collective-permute-start.2 = (bf16[1,1,192,4096]{3,2,1,0:T(8,128)(2,1)}, bf16[1,1,192,4096]{3,2,1,0:T(8,128)(2,1)}, u32[]{:S(2)}, u32[]{:S(2)}) collective-permute-start(bf16[1,1,192,4096]{3,2,1,0:T(8,128)(2,1)} %param.15), channel_id=1, source_target_pairs={{0,32},{4,36},{8,40},{12,44},{16,48},{20,52},{24,56},{28,60},{32,0... | collective-permute-start | bytes 4718600 | tf_op jit(solution)/shard_map/ppermute | solution.py:10
  30.0 261.8 %collective-permute-start.3 = (bf16[1,1,192,4096]{3,2,1,0:T(8,128)(2,1)}, bf16[1,1,192,4096]{3,2,1,0:T(8,128)(2,1)}, u32[]{:S(2)}, u32[]{:S(2)}) collective-permute-start(bf16[1,1,192,4096]{3,2,1,0:T(8,128)(2,1)} %param.16), channel_id=1, source_target_pairs={{0,32},{4,36},{8,40},{12,44},{16,48},{20,52},{24,56},{28,60},{32,0... | collective-permute-start | bytes 4718600 | tf_op jit(solution)/shard_map/ppermute | solution.py:10
  142.5 12.1 %copy-start.14 = (bf16[1,1,2,4096,768]{4,3,2,1,0:T(8,128)(2,1)S(1)}, bf16[1,1,2,4096,768]{4,3,2,1,0:T(8,128)(2,1)}, u32[]{:S(2)}) copy-start(bf16[1,1,2,4096,768]{4,3,2,1,0:T(8,128)(2,1)} %all-gather.3.cloned.1.call-done) | copy-start | bytes 37748740
  420.8 2.5 copy-start.5
  420.8 12.6 %collective-permute-start.4 = (bf16[64,4096]{1,0:T(8,128)(2,1)S(1)}, bf16[64,4096]{1,0:T(8,128)(2,1)S(1)}, u32[]{:S(2)}, u32[]{:S(2)}) collective-permute-start(bf16[64,4096]{1,0:T(8,128)(2,1)S(1)} %fusion.9), channel_id=1, source_target_pairs={{0,64},{1,65},{2,66},{3,67},{4,68},{5,69},{6,70},{7,71},{8,72},{9,... | collective-permute-start | bytes 1572872 | tf_op jit(solution)/shard_map/ppermute | solution.py:16
  434.7 0.8 copy-start.3
  440.0 101.6 %all-to-all-start.1 = ((bf16[16,64,4096]{2,1,0:T(8,128)(2,1)}), bf16[16,64,4096]{2,1,0:T(8,128)(2,1)}, u32[]{:S(2)}, u32[]{:S(2)}) async-start(bf16[16,64,4096]{2,1,0:T(8,128)(2,1)} %stack.12), calls=%async_computation.2 | async-start | bytes 16777216 | tf_op jit(solution)/shard_map/all_to_all | solution.py:59
  444.8 232.5 %reduce-scatter.5.cloned.1.call-start = ((), (), s32[]{:S(2)}) async-start(), calls=%async_computation.7 | async-start | bytes 8912896 | tf_op jit(solution)/shard_map/reduce_scatter | solution.py:74
  575.4 0.7 copy-start.15
  576.7 4.6 copy-start.1
  581.3 4.1 copy-start.7
  581.3 4.1 copy-start.8
  585.4 91.9 %copy-start.4 = (bf16[64,4096]{1,0:T(8,128)(2,1)S(1)}, bf16[64,4096]{1,0:T(8,128)(2,1)}, u32[]{:S(2)}) copy-start(bf16[64,4096]{1,0:T(8,128)(2,1)} %copy-done.3) | copy-start | bytes 1572868
  585.4 93.0 %copy-start.6 = (bf16[64,4096]{1,0:T(8,128)(2,1)S(1)}, bf16[64,4096]{1,0:T(8,128)(2,1)}, u32[]{:S(2)}) copy-start(bf16[64,4096]{1,0:T(8,128)(2,1)} %copy-done.5) | copy-start | bytes 1572868
Sparse Core Ops, SparseCore 0:
  9.7 121.0 all-gather.2
  132.5 66.6 all-gather.4
  292.0 127.4 reduce-scatter.2
  575.6 101.6 reduce-scatter.4
